TPU v7x, 32 devices: a whole 2x2x4 slice. The times are simulated.
32 devices in a mesh: dp: 4 (over y, x), seq: 8 (over z, core).
Axes of the slice: x: 2, y: 2, z: 4, core: 2. Of those that a mesh axis runs over, the one named last changes fastest.
Arguments:
- tokens: bfloat16 [4, 4, 512, 1024], P('dp', None, 'seq'), may hold values from -6 to 6
- norm1_gain: bfloat16 [1024], P('dp'), may hold values from 0.5 to 1.5
- w_query: bfloat16 [1024, 1024], P('dp'), may hold values from -0.1875 to 0.1875
- w_latent: bfloat16 [1024, 512], P('dp'), may hold values from -0.1875 to 0.1875
- w_key_up: bfloat16 [256, 1024], P('dp'), may hold values from -0.375 to 0.375
- w_value_up: bfloat16 [256, 1024], P('dp'), may hold values from -0.375 to 0.375
- w_out: bfloat16 [1024, 1024], P('dp'), may hold values from -1.5 to 1.5
- norm2_gain: bfloat16 [1024], P('dp'), may hold values from 0.5 to 1.5
- w_gate: bfloat16 [1024, 2816], P('dp'), may hold values from -0.1875 to 0.1875
- w_up: bfloat16 [1024, 2816], P('dp'), may hold values from -0.1875 to 0.1875
- w_down: bfloat16 [2816, 1024], P('dp'), may hold values from -0.109375 to 0.109375
- out_grad: bfloat16 [4, 4, 512, 1024], P('dp', None, 'seq'), may hold values from -6 to 6
- seq_lengths: int32 [4, 66], P('dp'), may hold values from 0 to 1024, as said below
Outputs:
- layer_out: bfloat16 [4, 4, 512, 1024], P('dp', None, 'seq')
- tokens_grad: bfloat16 [4, 4, 512, 1024], P('dp', None, 'seq')
- norm1_gain_grad: float32 [1024], P('dp')
- w_query_grad: float32 [1024, 1024], P('dp')
- w_latent_grad: float32 [1024, 512], P('dp')
- w_key_up_grad: float32 [256, 1024], P('dp')
- w_value_up_grad: float32 [256, 1024], P('dp')
- w_out_grad: float32 [1024, 1024], P('dp')
- norm2_gain_grad: float32 [1024], P('dp')
- w_gate_grad: float32 [1024, 2816], P('dp')
- w_up_grad: float32 [1024, 2816], P('dp')
- w_down_grad: float32 [2816, 1024], P('dp')
Inputs may be any that keep to these rules, and one draw needn't show every extreme that they name: `seq_lengths`: the entries of a stream sum to 2048. Even entries are sequence lengths; every stream holds one sequence of exactly 1024 positions. Odd entries are padding of at most 64 positions.
All inputs are finite; a program needn't handle non-finite values.
Results may differ from a plain program's by a relative error of at most 0.02.
Values may be sent and summed in bfloat16 or wider, within the bound.
No kernel may reach another device: no remote copies, remote signals or barrier semaphores. Data moves between devices by JAX's collectives and lax.ppermute only.
A program may use at most 256 MiB of HBM per device.

v0:
```python
import math

import jax
import jax.numpy as jnp
from jax import lax
from jax.sharding import PartitionSpec as P

HEADS = 16
HEAD_DIM = 64
GROUPS = 2
LATENT = 256
SEQ_MIN = 1024


NEG_FILL = -1e30
NORM_EPS = 1e-05


def rms_scale(values, gain):
    inverse = lax.rsqrt(jnp.mean(values * values, axis=-1, keepdims=True) + NORM_EPS)
    return values * inverse * gain


def swish_product(gate_vals, up_vals):
    return gate_vals * jax.nn.sigmoid(gate_vals) * up_vals


def seq_table(stretches):
    run_ends = jnp.cumsum(stretches)
    firsts = run_ends - stretches
    return (firsts[0::2], stretches[0::2])


def inside_table(starts, lengths, positions):
    return (positions[:, None] >= starts[None, :]) & (
        positions[:, None] < starts[None, :] + lengths[None, :]
    )


def label_rows(inside):
    labels = jnp.arange(1, inside.shape[1] + 1, dtype=jnp.int32)
    return jnp.sum(jnp.where(inside, labels[None, :], 0), axis=1)


def per_device(
    tokens,
    norm1_gain,
    w_query,
    w_latent,
    w_key_up,
    w_value_up,
    w_out,
    norm2_gain,
    w_gate,
    w_up,
    w_down,
    out_grad,
    seq_lengths,
):
    gathered = (
        lax.all_gather(norm1_gain, "dp", axis=0, tiled=True),
        lax.all_gather(w_query, "dp", axis=0, tiled=True),
        lax.all_gather(w_latent, "dp", axis=0, tiled=True),
        lax.all_gather(w_key_up, "dp", axis=0, tiled=True),
        lax.all_gather(w_value_up, "dp", axis=0, tiled=True),
        lax.all_gather(w_out, "dp", axis=0, tiled=True),
        lax.all_gather(norm2_gain, "dp", axis=0, tiled=True),
        lax.all_gather(w_gate, "dp", axis=0, tiled=True),
        lax.all_gather(w_up, "dp", axis=0, tiled=True),
        lax.all_gather(w_down, "dp", axis=0, tiled=True),
    )
    gain_one, query_w, latent_w, key_w, value_w, out_w, gain_two, gate_w, up_w, down_w = gathered
    piece_count = tokens.shape[1]
    block_rows = tokens.shape[2]
    row_width = tokens.shape[3]
    tok_rows = piece_count * block_rows
    my_index = lax.axis_index("seq")
    span_rows = block_rows * lax.axis_size("seq")
    longest = max(SEQ_MIN, span_rows)
    window = longest + block_rows
    stream_len = piece_count * span_rows
    latent_width = GROUPS * LATENT
    per_group = HEADS // GROUPS
    score_scale = 1.0 / math.sqrt(HEAD_DIM)
    seq_first, seq_len = seq_table(seq_lengths[0])
    row_pos = (
        jnp.arange(piece_count, dtype=jnp.int32)[:, None] * span_rows
        + my_index * block_rows
        + jnp.arange(block_rows, dtype=jnp.int32)[None, :]
    )
    row_labels = label_rows(inside_table(seq_first, seq_len, row_pos.reshape(-1))).reshape(
        piece_count, block_rows
    )
    key_first = jnp.maximum(row_pos[:, 0] + block_rows - window, 0)
    key_pos = key_first[:, None] + jnp.arange(window, dtype=jnp.int32)[None, :]
    key_labels = label_rows(inside_table(seq_first, seq_len, key_pos.reshape(-1))).reshape(
        piece_count, window
    )
    same_seq = (
        (row_labels[:, :, None] == key_labels[:, None, :])
        & (row_labels[:, :, None] > 0)
        & (key_pos[:, None, :] <= row_pos[:, :, None])
    )
    masks = same_seq | (key_pos[:, None, :] == row_pos[:, :, None])

    def windows_of(stream_vals):
        return jnp.stack(
            [
                lax.dynamic_slice_in_dim(stream_vals, key_first[piece_id], window, 0)
                for piece_id in range(piece_count)
            ]
        )

    tok_float = tokens[0].reshape(tok_rows, row_width).astype(jnp.float32)
    gain_one_f = gain_one.astype(jnp.float32)
    gain_two_f = gain_two.astype(jnp.float32)
    normed = rms_scale(tok_float, gain_one_f).astype(jnp.bfloat16)
    queries = jnp.dot(normed, query_w, preferred_element_type=jnp.float32).astype(jnp.bfloat16)
    latent = jnp.dot(normed, latent_w, preferred_element_type=jnp.float32).astype(jnp.bfloat16)
    key_up = key_w.reshape(LATENT, HEADS, HEAD_DIM)
    value_up = value_w.reshape(LATENT, HEADS, HEAD_DIM)
    query_heads = queries.reshape(tok_rows, HEADS, HEAD_DIM)
    absorbed = jnp.einsum(
        "thd,chd->thc", query_heads, key_up, preferred_element_type=jnp.float32
    ).astype(jnp.bfloat16)
    absorbed_p = absorbed.reshape(piece_count, block_rows, HEADS, LATENT)
    latent_pieces = latent.reshape(piece_count, block_rows, latent_width)
    whole_stream = lax.all_gather(latent_pieces, "seq", axis=1, tiled=True).reshape(
        stream_len, latent_width
    )
    key_blocks = windows_of(whole_stream)

    def group_scores(keys_p, group_id):
        head_span = slice(group_id * per_group, (group_id + 1) * per_group)
        group_queries = absorbed_p[:, :, head_span, :]
        group_keys = keys_p[:, :, group_id * LATENT : (group_id + 1) * LATENT]
        scores = (
            jnp.einsum(
                "pthc,pkc->pthk", group_queries, group_keys, preferred_element_type=jnp.float32
            )
            * score_scale
        )
        return (group_queries, group_keys, jnp.where(masks[:, :, None, :], scores, NEG_FILL))

    log_parts = []
    mixed_parts = []
    for group_id in range(GROUPS):
        group_keys, scores = group_scores(key_blocks, group_id)[1:]
        row_top = jnp.max(scores, axis=-1)
        group_log = row_top + jnp.log(jnp.sum(jnp.exp(scores - row_top[..., None]), axis=-1))
        prob_vals = jnp.exp(scores - group_log[..., None]).astype(jnp.bfloat16)
        mixed_parts.append(
            jnp.einsum("pthk,pkc->pthc", prob_vals, group_keys, preferred_element_type=jnp.float32)
        )
        log_parts.append(group_log)
    log_total = jnp.concatenate(log_parts, axis=2)
    mixed_latent = jnp.concatenate(mixed_parts, axis=2).reshape(tok_rows, HEADS, LATENT)
    mixed_round = mixed_latent.astype(jnp.bfloat16)
    heads_out = (
        jnp.einsum("thc,chd->thd", mixed_round, value_up, preferred_element_type=jnp.float32)
        .astype(jnp.bfloat16)
        .reshape(tok_rows, HEADS * HEAD_DIM)
    )
    resid = tok_float + jnp.dot(heads_out, out_w, preferred_element_type=jnp.float32)
    normed_two = rms_scale(resid, gain_two_f).astype(jnp.bfloat16)
    gate_vals = jnp.dot(normed_two, gate_w, preferred_element_type=jnp.float32)
    up_vals = jnp.dot(normed_two, up_w, preferred_element_type=jnp.float32)
    hidden = swish_product(gate_vals, up_vals).astype(jnp.bfloat16)
    layer_out = (resid + jnp.dot(hidden, down_w, preferred_element_type=jnp.float32)).astype(
        jnp.bfloat16
    )
    grad_round = out_grad[0].reshape(tok_rows, row_width)
    grad_float = grad_round.astype(jnp.float32)
    down_grad = jnp.einsum("tf,td->fd", hidden, grad_round, preferred_element_type=jnp.float32)
    d_hidden = jnp.einsum("td,fd->tf", grad_round, down_w, preferred_element_type=jnp.float32)
    swish_pull = jax.vjp(swish_product, gate_vals, up_vals)[1]
    d_gate, d_up = swish_pull(d_hidden)
    d_gate = d_gate.astype(jnp.bfloat16)
    d_up = d_up.astype(jnp.bfloat16)
    gate_grad = jnp.einsum("td,tf->df", normed_two, d_gate, preferred_element_type=jnp.float32)
    up_grad = jnp.einsum("td,tf->df", normed_two, d_up, preferred_element_type=jnp.float32)
    d_normed_two = jnp.einsum(
        "tf,df->td", d_gate, gate_w, preferred_element_type=jnp.float32
    ) + jnp.einsum("tf,df->td", d_up, up_w, preferred_element_type=jnp.float32)
    norm_two_pull = jax.vjp(rms_scale, resid, gain_two_f)[1]
    d_resid_norm, gain_two_grad = norm_two_pull(d_normed_two)
    d_resid = grad_float + d_resid_norm
    d_resid_round = d_resid.astype(jnp.bfloat16)
    out_w_grad = jnp.einsum(
        "te,td->ed", heads_out, d_resid_round, preferred_element_type=jnp.float32
    )
    d_heads = (
        jnp.einsum("td,ed->te", d_resid_round, out_w, preferred_element_type=jnp.float32)
        .astype(jnp.bfloat16)
        .reshape(tok_rows, HEADS, HEAD_DIM)
    )
    value_grad = jnp.einsum(
        "thc,thd->chd", mixed_round, d_heads, preferred_element_type=jnp.float32
    ).reshape(LATENT, HEADS * HEAD_DIM)
    d_mixed = jnp.einsum(
        "thd,chd->thc", d_heads, value_up, preferred_element_type=jnp.float32
    ).astype(jnp.bfloat16)
    delta = jnp.sum(d_mixed.astype(jnp.float32) * mixed_latent, axis=-1)
    d_mixed_p = d_mixed.reshape(piece_count, block_rows, HEADS, LATENT)
    delta_p = delta.reshape(piece_count, block_rows, HEADS)
    again_stream = lax.all_gather(latent_pieces, "seq", axis=1, tiled=True).reshape(
        stream_len, latent_width
    )
    back_blocks = windows_of(again_stream)
    absorbed_parts = []
    key_parts = []
    for group_id in range(GROUPS):
        head_span = slice(group_id * per_group, (group_id + 1) * per_group)
        group_queries, group_keys, scores = group_scores(back_blocks, group_id)
        prob_vals = jnp.exp(scores - log_total[:, :, head_span, None])
        group_grads = d_mixed_p[:, :, head_span, :]
        d_probs = jnp.einsum(
            "pthc,pkc->pthk", group_grads, group_keys, preferred_element_type=jnp.float32
        )
        d_scores = (prob_vals * (d_probs - delta_p[:, :, head_span, None])).astype(jnp.bfloat16)
        absorbed_parts.append(
            jnp.einsum("pthk,pkc->pthc", d_scores, group_keys, preferred_element_type=jnp.float32)
        )
        key_terms = score_scale * jnp.einsum(
            "pthk,pthc->pkc", d_scores, group_queries, preferred_element_type=jnp.float32
        )
        key_terms = key_terms + jnp.einsum(
            "pthk,pthc->pkc",
            prob_vals.astype(jnp.bfloat16),
            group_grads,
            preferred_element_type=jnp.float32,
        )
        key_parts.append(key_terms)
    d_abs_sum = jnp.concatenate(absorbed_parts, axis=2).reshape(tok_rows, HEADS, LATENT)
    window_grads = jnp.concatenate(key_parts, axis=2)
    grad_term = jnp.zeros((stream_len, latent_width), jnp.float32)
    for piece_id in range(piece_count):
        current = lax.dynamic_slice_in_dim(grad_term, key_first[piece_id], window, 0)
        grad_term = lax.dynamic_update_slice_in_dim(
            grad_term, current + window_grads[piece_id], key_first[piece_id], 0
        )
    latent_total = lax.psum_scatter(
        grad_term.reshape(piece_count, span_rows, latent_width),
        "seq",
        scatter_dimension=1,
        tiled=True,
    ).reshape(tok_rows, latent_width)
    d_absorbed = (score_scale * d_abs_sum).astype(jnp.bfloat16)
    key_grad = jnp.einsum(
        "thc,thd->chd", d_absorbed, query_heads, preferred_element_type=jnp.float32
    ).reshape(LATENT, HEADS * HEAD_DIM)
    d_queries = (
        jnp.einsum("thc,chd->thd", d_absorbed, key_up, preferred_element_type=jnp.float32)
        .astype(jnp.bfloat16)
        .reshape(tok_rows, HEADS * HEAD_DIM)
    )
    d_latent = latent_total.astype(jnp.bfloat16)
    query_grad = jnp.einsum("td,te->de", normed, d_queries, preferred_element_type=jnp.float32)
    latent_grad = jnp.einsum("td,te->de", normed, d_latent, preferred_element_type=jnp.float32)
    d_normed = jnp.einsum(
        "te,de->td", d_queries, query_w, preferred_element_type=jnp.float32
    ) + jnp.einsum("te,de->td", d_latent, latent_w, preferred_element_type=jnp.float32)
    norm_one_pull = jax.vjp(rms_scale, tok_float, gain_one_f)[1]
    d_tok_norm, gain_one_grad = norm_one_pull(d_normed)
    tokens_grad = (d_resid + d_tok_norm).astype(jnp.bfloat16)
    grads = (
        gain_one_grad,
        query_grad,
        latent_grad,
        key_grad,
        value_grad,
        out_w_grad,
        gain_two_grad,
        gate_grad,
        up_grad,
        down_grad,
    )
    shares = (
        lax.psum_scatter(
            grads[0].astype(jnp.bfloat16), "dp", scatter_dimension=0, tiled=True
        ).astype(jnp.float32),
        lax.psum_scatter(
            grads[1].astype(jnp.bfloat16), "dp", scatter_dimension=0, tiled=True
        ).astype(jnp.float32),
        lax.psum_scatter(
            grads[2].astype(jnp.bfloat16), "dp", scatter_dimension=0, tiled=True
        ).astype(jnp.float32),
        lax.psum_scatter(
            grads[3].astype(jnp.bfloat16), "dp", scatter_dimension=0, tiled=True
        ).astype(jnp.float32),
        lax.psum_scatter(
            grads[4].astype(jnp.bfloat16), "dp", scatter_dimension=0, tiled=True
        ).astype(jnp.float32),
        lax.psum_scatter(
            grads[5].astype(jnp.bfloat16), "dp", scatter_dimension=0, tiled=True
        ).astype(jnp.float32),
        lax.psum_scatter(
            grads[6].astype(jnp.bfloat16), "dp", scatter_dimension=0, tiled=True
        ).astype(jnp.float32),
        lax.psum_scatter(
            grads[7].astype(jnp.bfloat16), "dp", scatter_dimension=0, tiled=True
        ).astype(jnp.float32),
        lax.psum_scatter(
            grads[8].astype(jnp.bfloat16), "dp", scatter_dimension=0, tiled=True
        ).astype(jnp.float32),
        lax.psum_scatter(
            grads[9].astype(jnp.bfloat16), "dp", scatter_dimension=0, tiled=True
        ).astype(jnp.float32),
    )
    summed = lax.psum(
        (
            shares[0],
            shares[1],
            shares[2],
            shares[3],
            shares[4],
            shares[5],
            shares[6],
            shares[7],
            shares[8],
            shares[9],
        ),
        "seq",
    )
    return (
        layer_out.reshape(1, piece_count, block_rows, row_width),
        tokens_grad.reshape(1, piece_count, block_rows, row_width),
        summed[0],
        summed[1],
        summed[2],
        summed[3],
        summed[4],
        summed[5],
        summed[6],
        summed[7],
        summed[8],
        summed[9],
    )


def solution(mesh):
    in_specs = (
        P("dp", None, "seq", None),
        P("dp"),
        P("dp", None),
        P("dp", None),
        P("dp", None),
        P("dp", None),
        P("dp", None),
        P("dp"),
        P("dp", None),
        P("dp", None),
        P("dp", None),
        P("dp", None, "seq", None),
        P("dp", None),
    )
    out_specs = (
        P("dp", None, "seq", None),
        P("dp", None, "seq", None),
        P("dp"),
        P("dp", None),
        P("dp", None),
        P("dp", None),
        P("dp", None),
        P("dp", None),
        P("dp"),
        P("dp", None),
        P("dp", None),
        P("dp", None),
    )
    return jax.shard_map(
        per_device, mesh=mesh, in_specs=in_specs, out_specs=out_specs, check_vma=False
    )
```

profile of v0, /device:TPU:0, one launch (start us, length us, event | category | flops | bytes accessed | tf_op | source)
XLA Modules:
  0.0 1120.6 jit_solution(5432038570921758720)
XLA Ops:
  11.3 9.5 all-gather
  22.1 17.1 %all-gather.12.cloned.1.call-done = bf16[1024,512]{1,0:T(8,128)(2,1)} async-done(((bf16[256,512]{1,0:T(8,128)(2,1)}), bf16[1024,512]{1,0:T(8,128)(2,1)}) %all-gather.12.cloned.1.call-update) | async-done | bytes 1048592 | tf_op jit(solution)/shard_map/all_gather | solution.py:63
  46.3 14.0 %all_gather.36 = bf16[256,1024]{1,0:T(8,128)(2,1)S(1)} all-gather(bf16[64,1024]{1,0:T(8,128)(2,1)S(1)} %copy-done.40), channel_id=1, replica_groups=mesh['dp'=4,'seq'=8] {'dp'}, dimensions={0}, use_global_device_ids=true | all-gather | bytes 655360 | tf_op jit(solution)/shard_map/all_gather | solution.py:64
  60.8 12.0 %all_gather.39 = bf16[256,1024]{1,0:T(8,128)(2,1)S(1)} all-gather(bf16[64,1024]{1,0:T(8,128)(2,1)S(1)} %copy-done.41), channel_id=1, replica_groups=mesh['dp'=4,'seq'=8] {'dp'}, dimensions={0}, use_global_device_ids=true | all-gather | bytes 655360 | tf_op jit(solution)/shard_map/all_gather | solution.py:65
  79.2 8.8 all-gather.1
  94.2 18.0 %all-gather.14.cloned.1.call-done = bf16[4,512,512]{2,1,0:T(8,128)(2,1)} async-done(((bf16[4,64,512]{2,1,0:T(8,128)(2,1)}), bf16[4,512,512]{2,1,0:T(8,128)(2,1)}) %all-gather.14.cloned.1.call-update) | async-done | bytes 2097168 | tf_op jit(solution)/shard_map/all_gather | solution.py:128
  140.6 8.2 all-gather.16.cloned.1.call-done
  151.4 64.9 %all-gather.18.cloned.1.call-done = bf16[1024,2816]{1,0:T(8,128)(2,1)} async-done(((bf16[256,2816]{1,0:T(8,128)(2,1)}), bf16[1024,2816]{1,0:T(8,128)(2,1)}) %all-gather.18.cloned.1.call-update) | async-done | bytes 5767184 | tf_op jit(solution)/shard_map/all_gather | solution.py:68
  222.2 61.7 %all-gather.20.cloned.1.call-done = bf16[1024,2816]{1,0:T(8,128)(2,1)} async-done(((bf16[256,2816]{1,0:T(8,128)(2,1)}), bf16[1024,2816]{1,0:T(8,128)(2,1)}) %all-gather.20.cloned.1.call-update) | async-done | bytes 5767184 | tf_op jit(solution)/shard_map/all_gather | solution.py:69
  289.7 61.8 %all-gather.22.cloned.1.call-done = bf16[2816,1024]{1,0:T(8,128)(2,1)} async-done(((bf16[704,1024]{1,0:T(8,128)(2,1)}), bf16[2816,1024]{1,0:T(8,128)(2,1)}) %all-gather.22.cloned.1.call-update) | async-done | bytes 5767184 | tf_op jit(solution)/shard_map/all_gather | solution.py:70
  351.5 9.5 multiply_convert_fusion.2
  377.9 6.8 multiply_convert_fusion
  391.0 8.1 bitcast_add_fusion
  411.4 7.5 bitcast_add_fusion.1
  485.7 23.7 %reduce-scatter.10.cloned.1.call-done = f32[4,64,512]{2,1,0:T(8,128)} async-done(((f32[4,512,512]{2,1,0:T(8,128)}), f32[4,64,512]{2,1,0:T(8,128)}) %reduce-scatter.10.cloned.1.call-update) | async-done | bytes 524304 | tf_op jit(solution)/shard_map/reduce_scatter | solution.py:242
  540.9 22.0 %reduce-scatter.16.cloned.1.call-done = bf16[64,1024]{1,0:T(8,128)(2,1)} async-done(((bf16[256,1024]{1,0:T(8,128)(2,1)}), bf16[64,1024]{1,0:T(8,128)(2,1)}) %reduce-scatter.16.cloned.1.call-update) | async-done | bytes 131088 | tf_op jit(solution)/shard_map/reduce_scatter | solution.py:288
  562.8 38.8 %reduce-scatter.20.cloned.1.call-done = bf16[256,1024]{1,0:T(8,128)(2,1)} async-done(((bf16[1024,1024]{1,0:T(8,128)(2,1)}), bf16[256,1024]{1,0:T(8,128)(2,1)}) %reduce-scatter.20.cloned.1.call-update) | async-done | bytes 524304 | tf_op jit(solution)/shard_map/reduce_scatter | solution.py:294
  601.6 38.9 %reduce-scatter.12.cloned.1.call-done = bf16[256,1024]{1,0:T(8,128)(2,1)} async-done(((bf16[1024,1024]{1,0:T(8,128)(2,1)}), bf16[256,1024]{1,0:T(8,128)(2,1)}) %reduce-scatter.12.cloned.1.call-update) | async-done | bytes 524304 | tf_op jit(solution)/shard_map/reduce_scatter | solution.py:282
  642.7 8.9 all-reduce.3
  652.8 18.3 %reduce-scatter.14.cloned.1.call-done = bf16[256,512]{1,0:T(8,128)(2,1)} async-done(((bf16[1024,512]{1,0:T(8,128)(2,1)}), bf16[256,512]{1,0:T(8,128)(2,1)}) %reduce-scatter.14.cloned.1.call-update) | async-done | bytes 262160 | tf_op jit(solution)/shard_map/reduce_scatter | solution.py:285
  671.1 69.0 %reduce-scatter.22.cloned.1.call-done = bf16[256,2816]{1,0:T(8,128)(2,1)} async-done(((bf16[1024,2816]{1,0:T(8,128)(2,1)}), bf16[256,2816]{1,0:T(8,128)(2,1)}) %reduce-scatter.22.cloned.1.call-update) | async-done | bytes 1441808 | tf_op jit(solution)/shard_map/reduce_scatter | solution.py:300
  740.1 68.9 %reduce-scatter.24.cloned.1.call-done = bf16[256,2816]{1,0:T(8,128)(2,1)} async-done(((bf16[1024,2816]{1,0:T(8,128)(2,1)}), bf16[256,2816]{1,0:T(8,128)(2,1)}) %reduce-scatter.24.cloned.1.call-update) | async-done | bytes 1441808 | tf_op jit(solution)/shard_map/reduce_scatter | solution.py:303
  809.1 68.9 %reduce-scatter.26.cloned.1.call-done = bf16[704,1024]{1,0:T(8,128)(2,1)} async-done(((bf16[2816,1024]{1,0:T(8,128)(2,1)}), bf16[704,1024]{1,0:T(8,128)(2,1)}) %reduce-scatter.26.cloned.1.call-update) | async-done | bytes 1441808 | tf_op jit(solution)/shard_map/reduce_scatter | solution.py:306
  878.0 235.7 %all-reduce.5 = (f32[256]{0:T(256)}, f32[256,1024]{1,0:T(8,128)}, f32[256,512]{1,0:T(8,128)}, f32[64,1024]{1,0:T(8,128)}, f32[64,1024]{1,0:T(8,128)}, /*index=5*...) all-reduce(f32[256]{0:T(256)S(1)} %get-tuple-element.60, ...), channel_id=1, replica_groups=mesh['dp'=4,'seq'=8] {'seq'}, use_global_device_ids=true, to_apply=%region_15.16 | all-reduce | flops 2949632 | bytes 17698816 | tf_op jit(solution)/shard_map/psum | solution.py:310
  (252 shorter events, 196.0 us)
Async XLA Ops:
  7.2 32.0 %all-gather.12.cloned.1.call-start = ((), (), s32[]{:S(2)}) async-start(), calls=%async_computation.10 | async-start | bytes 1310720 | tf_op jit(solution)/shard_map/all_gather | solution.py:63
  7.9 82.7 %all-gather.10.cloned.1.call-start = ((), (), s32[]{:S(2)}) async-start(), calls=%async_computation.9 | async-start | bytes 2621440 | tf_op jit(solution)/shard_map/all_gather | solution.py:62
  8.7 103.6 %all-gather.14.cloned.1.call-start = ((), (), s32[]{:S(2)}) async-start(), calls=%async_computation.11 | async-start | bytes 2359296 | tf_op jit(solution)/shard_map/all_gather | solution.py:128
  41.6 107.2 %all-gather.16.cloned.1.call-start = ((), (), s32[]{:S(2)}) async-start(), calls=%async_computation.12 | async-start | bytes 2621440 | tf_op jit(solution)/shard_map/all_gather | solution.py:66
  42.2 174.1 %all-gather.18.cloned.1.call-start = ((), (), s32[]{:S(2)}) async-start(), calls=%async_computation.13 | async-start | bytes 7208960 | tf_op jit(solution)/shard_map/all_gather | solution.py:68
  42.8 241.1 %all-gather.20.cloned.1.call-start = ((), (), s32[]{:S(2)}) async-start(), calls=%async_computation.14 | async-start | bytes 7208960 | tf_op jit(solution)/shard_map/all_gather | solution.py:69
  43.4 308.2 %all-gather.22.cloned.1.call-start = ((), (), s32[]{:S(2)}) async-start(), calls=%async_computation.15 | async-start | bytes 7208960 | tf_op jit(solution)/shard_map/all_gather | solution.py:70
  44.1 465.2 %reduce-scatter.10.cloned.1.call-start = ((), (), s32[]{:S(2)}) async-start(), calls=%async_computation.16 | async-start | bytes 4718592 | tf_op jit(solution)/shard_map/reduce_scatter | solution.py:242
  151.2 217.6 %copy-start.11 = (f32[256,1024]{1,0:T(8,128)}, f32[256,1024]{1,0:T(8,128)S(1)}, u32[]{:S(2)}) copy-start(f32[256,1024]{1,0:T(8,128)S(1)} %get-tuple-element.54) | copy-start | bytes 3145732
  151.4 132.5 %copy-start.17 = (bf16[256,1024]{1,0:T(8,128)(2,1)}, bf16[256,1024]{1,0:T(8,128)(2,1)S(1)}, u32[]{:S(2)}) copy-start(bf16[256,1024]{1,0:T(8,128)(2,1)S(1)} %multiply_convert_fusion.4) | copy-start | bytes 1572868
  222.2 129.3 %copy-start.31 = (bf16[1,4,64,1024]{3,2,1,0:T(8,128)(2,1)S(1)}, bf16[1,4,64,1024]{3,2,1,0:T(8,128)(2,1)}, u32[]{:S(2)}) copy-start(bf16[1,4,64,1024]{3,2,1,0:T(8,128)(2,1)} %param.24) | copy-start | bytes 1572868
  459.1 81.7 %reduce-scatter.18.cloned.1.call-start = ((), (), s32[]{:S(2)}) async-start(), calls=%async_computation.20 | async-start | bytes 655360 | tf_op jit(solution)/shard_map/reduce_scatter | solution.py:291
  464.8 98.0 %reduce-scatter.16.cloned.1.call-start = ((), (), s32[]{:S(2)}) async-start(), calls=%async_computation.19 | async-start | bytes 655360 | tf_op jit(solution)/shard_map/reduce_scatter | solution.py:288
  477.9 123.7 %reduce-scatter.20.cloned.1.call-start = ((), (), s32[]{:S(2)}) async-start(), calls=%async_computation.21 | async-start | bytes 2621440 | tf_op jit(solution)/shard_map/reduce_scatter | solution.py:294
  480.0 160.5 %reduce-scatter.12.cloned.1.call-start = ((), (), s32[]{:S(2)}) async-start(), calls=%async_computation.17 | async-start | bytes 2621440 | tf_op jit(solution)/shard_map/reduce_scatter | solution.py:282
  485.6 185.5 %reduce-scatter.14.cloned.1.call-start = ((), (), s32[]{:S(2)}) async-start(), calls=%async_computation.18 | async-start | bytes 1310720 | tf_op jit(solution)/shard_map/reduce_scatter | solution.py:285
  511.9 228.3 %reduce-scatter.22.cloned.1.call-start = ((), (), s32[]{:S(2)}) async-start(), calls=%async_computation.22 | async-start | bytes 7208960 | tf_op jit(solution)/shard_map/reduce_scatter | solution.py:300
  517.8 291.3 %reduce-scatter.24.cloned.1.call-start = ((), (), s32[]{:S(2)}) async-start(), calls=%async_computation.23 | async-start | bytes 7208960 | tf_op jit(solution)/shard_map/reduce_scatter | solution.py:303
  523.4 354.6 %reduce-scatter.26.cloned.1.call-start = ((), (), s32[]{:S(2)}) async-start(), calls=%async_computation.24 | async-start | bytes 7208960 | tf_op jit(solution)/shard_map/reduce_scatter | solution.py:306
  535.3 105.2 %copy-start.47 = (f32[256]{0:T(256)S(1)}, f32[256]{0:T(256)}, u32[]{:S(2)}) copy-start(f32[256]{0:T(256)} %copy-done.46) | copy-start | bytes 3076
  535.3 107.4 %copy-start.51 = (bf16[1024]{0:T(1024)(128)(2,1)S(1)}, bf16[1024]{0:T(1024)(128)(2,1)}, u32[]{:S(2)}) copy-start(bf16[1024]{0:T(1024)(128)(2,1)} %get-tuple-element.12) | copy-start | bytes 6148
  535.3 116.4 %copy-start.49 = (f32[256]{0:T(256)S(1)}, f32[256]{0:T(256)}, u32[]{:S(2)}) copy-start(f32[256]{0:T(256)} %copy-done.48) | copy-start | bytes 3076
  540.9 337.1 %copy-start.42 = (bf16[64,1024]{1,0:T(8,128)(2,1)S(1)}, bf16[64,1024]{1,0:T(8,128)(2,1)}, u32[]{:S(2)}) copy-start(bf16[64,1024]{1,0:T(8,128)(2,1)} %reduce-scatter.18.cloned.1.call-done) | copy-start | bytes 393220
  562.8 315.2 %copy-start.43 = (bf16[64,1024]{1,0:T(8,128)(2,1)S(1)}, bf16[64,1024]{1,0:T(8,128)(2,1)}, u32[]{:S(2)}) copy-start(bf16[64,1024]{1,0:T(8,128)(2,1)} %reduce-scatter.16.cloned.1.call-done) | copy-start | bytes 393220
  (51 other events, 615.3 us)
Sparse Core Ops, SparseCore 0:
  9.9 29.3 all-gather.11
  41.1 39.8 all-gather.9
  83.1 29.1 all-gather.13
  113.9 34.8 all-gather.15
  150.5 65.7 all-gather.17
  218.0 65.7 all-gather.19
  285.7 65.7 all-gather.21
  459.3 50.0 reduce-scatter.9
  512.1 22.9 reduce-scatter.17
  538.0 24.7 reduce-scatter.15
  566.4 35.1 reduce-scatter.19
  605.3 35.1 reduce-scatter.11
  643.4 27.7 reduce-scatter.13
  674.3 65.8 reduce-scatter.21
  743.2 65.7 reduce-scatter.23
  812.2 65.7 reduce-scatter.25
where the time goes:
time: 1130 us; the launch traced here: 1120 us
  waiting for transfers between devices  584 us (52%)
  blocking collectives  289 us (26%)
  matrix products  145 us (13%)
  local copies, waits for them, and re-layouts  51.7 us (5%)
  other arithmetic  26.2 us (2%)
  between operations  23.8 us (2%)
    psum x1, blocking collectives, per_device(): lax.psum((shares[0], shares[1], shares[2], shares[3], shares[4], shares[5...  236 us
    reduce_scatter x1, waiting for transfers between devices, per_device(): lax.psum_scatter(grads[7].astype(jnp.bfloat16), 'dp', scatter_dimension=0...  69 us
    reduce_scatter x1, waiting for transfers between devices, per_device(): lax.psum_scatter(grads[9].astype(jnp.bfloat16), 'dp', scatter_dimension=0...  68.9 us
    reduce_scatter x1, waiting for transfers between devices, per_device(): lax.psum_scatter(grads[8].astype(jnp.bfloat16), 'dp', scatter_dimension=0...  68.9 us
    all_gather x1, waiting for transfers between devices, per_device(): lax.all_gather(w_gate, 'dp', axis=0, tiled=True)  64.9 us
    all_gather x1, waiting for transfers between devices, per_device(): lax.all_gather(w_down, 'dp', axis=0, tiled=True)  61.8 us
    all_gather x1, waiting for transfers between devices, per_device(): lax.all_gather(w_up, 'dp', axis=0, tiled=True)  61.7 us
    reduce_scatter x1, waiting for transfers between devices, per_device(): lax.psum_scatter(grads[1].astype(jnp.bfloat16), 'dp', scatter_dimension=0...  38.9 us
  transfers between devices with their start and end apart: 16, of which 14 were waited for; matrix products, arithmetic and copies ran while one was open for 10% of the time, Pallas kernels for 0%

commit v1 on v0

v1 whole, which is shorter than its diff:
```python
import functools
import math

import jax
import jax.numpy as jnp
from jax import lax
from jax.experimental import pallas as pl
from jax.experimental.pallas import tpu as pltpu
from jax.sharding import Mesh
from jax.sharding import PartitionSpec as P

HEADS = 16
HEAD_DIM = 64
GROUPS = 2
LATENT = 256
PER_GROUP = HEADS // GROUPS
GROUP_COLS = PER_GROUP * HEAD_DIM
KEY_BLOCK = 256
SCALE = 1.0 / math.sqrt(HEAD_DIM)
NEG_FILL = -1e30
NORM_EPS = 1e-05
F32 = jnp.float32
BF16 = jnp.bfloat16
DP = "dp"
SEQ = ("z", "core")
CHIP = ("dp", "core")


def mm(a, b):
    return jnp.dot(a, b, preferred_element_type=F32)


def mm_nt(a, b):
    return lax.dot_general(a, b, (((1,), (1,)), ((), ())), preferred_element_type=F32)


def mm_tn(a, b):
    return lax.dot_general(a, b, (((0,), (0,)), ((), ())), preferred_element_type=F32)


def low_lanes(rows):
    return lax.broadcasted_iota(jnp.int32, (rows, 2 * HEAD_DIM), 1) < HEAD_DIM


def pair_cols(pair):
    return slice(2 * HEAD_DIM * pair, 2 * HEAD_DIM * (pair + 1))


def expand_heads(vals, up_proj):
    low = low_lanes(vals.shape[0])
    out = []
    for pair in range(PER_GROUP // 2):
        part = vals[:, pair_cols(pair)]
        proj = up_proj[:, pair_cols(pair)]
        zero = jnp.zeros_like(part)
        out.append(mm_nt(jnp.where(low, part, zero), proj))
        out.append(mm_nt(jnp.where(low, zero, part), proj))
    return out


def shrink_heads(parts, up_proj):
    low = low_lanes(parts[0].shape[0])
    out = []
    for pair in range(PER_GROUP // 2):
        proj = up_proj[:, pair_cols(pair)]
        out.append(jnp.where(low, mm(parts[2 * pair], proj), mm(parts[2 * pair + 1], proj)))
    return jnp.concatenate(out, axis=1)


def outer_heads(parts, vals):
    low = low_lanes(LATENT)
    out = []
    for pair in range(PER_GROUP // 2):
        part = vals[:, pair_cols(pair)]
        out.append(jnp.where(low, mm_tn(parts[2 * pair], part), mm_tn(parts[2 * pair + 1], part)))
    return jnp.concatenate(out, axis=1)


def load_keys(lat_ref, slot_ref, block, strips, per_piece):
    piece = block // per_piece
    first = (block - piece * per_piece) * strips
    parts = [lat_ref[slot_ref[first + i], piece] for i in range(strips)]
    return jnp.concatenate(parts, axis=0), piece, first


def visible(block, base, starts, rows):
    row_pos = base + lax.broadcasted_iota(jnp.int32, (rows, KEY_BLOCK), 0)
    key_pos = block * KEY_BLOCK + lax.broadcasted_iota(jnp.int32, (rows, KEY_BLOCK), 1)
    return (key_pos >= starts) & (key_pos <= row_pos)


def masked(scores, seen, rows):
    tall = scores.shape[0]
    split = scores.reshape(PER_GROUP, rows, KEY_BLOCK)
    return jnp.where(seen[None], split, NEG_FILL).reshape(tall, KEY_BLOCK)


def forward_body(
    first_piece, lo_ref, hi_ref, base_ref, slot_ref, start_ref, lat_ref, query_ref, key_up_ref, value_up_ref,
    abs_ref, mixed_ref, lse_ref, out_ref, top_ref, sum_ref, acc_ref,
):
    piece_id = pl.program_id(1) + first_piece
    nseq, _, strip, _ = lat_ref.shape
    rows = query_ref.shape[0]
    strips = KEY_BLOCK // strip
    per_piece = nseq // strips
    for head, part in enumerate(expand_heads(query_ref[...], key_up_ref[...])):
        abs_ref[0, 0, head] = part.astype(BF16) * jnp.asarray(SCALE, BF16)
    tall = PER_GROUP * rows
    top_ref[...] = jnp.full(top_ref.shape, NEG_FILL, F32)
    sum_ref[...] = jnp.zeros(sum_ref.shape, F32)
    acc_ref[...] = jnp.zeros(acc_ref.shape, F32)
    starts = jnp.broadcast_to(start_ref[0][:, 0:1], (rows, KEY_BLOCK))

    def step(block, carry):
        keys, _, _ = load_keys(lat_ref, slot_ref, block, strips, per_piece)
        seen = visible(block, base_ref[piece_id], starts, rows)
        scores = masked(mm_nt(abs_ref[0, 0].reshape(tall, LATENT), keys), seen, rows)
        old_top = top_ref[...]
        new_top = jnp.maximum(old_top, jnp.max(scores, axis=1, keepdims=True))
        shrink = jnp.exp(old_top - new_top)
        probs = jnp.exp(scores - new_top)
        top_ref[...] = new_top
        sum_ref[...] = sum_ref[...] * shrink + jnp.sum(probs, axis=1, keepdims=True)
        acc_ref[...] = acc_ref[...] * shrink + mm(probs.astype(BF16), keys)
        return carry

    lax.fori_loop(lo_ref[piece_id], hi_ref[piece_id], step, 0)
    total = sum_ref[...]
    lse_ref[0, 0] = jnp.broadcast_to(top_ref[...] + jnp.log(total), (tall, 128))
    mixed = (acc_ref[...] * (1.0 / total)).astype(BF16).reshape(PER_GROUP, rows, LATENT)
    mixed_ref[0, 0] = mixed
    out_ref[...] = shrink_heads([mixed[h] for h in range(PER_GROUP)], value_up_ref[...]).astype(BF16)


def backward_body(
    first_piece, carried, *refs,
):
    refs = list(refs)
    lo_ref, hi_ref, base_ref, slot_ref, start_ref, lat_ref, query_ref, key_up_ref, value_up_ref = refs[:9]
    abs_ref, mixed_ref, lse_ref, grad_ref = refs[9:13]
    rest = refs[13:]
    if carried:
        carry_ref, dquery_ref, dlat_ref, key_grad_ref, value_grad_ref = rest[:5]
    else:
        dquery_ref, dlat_ref, carry_ref, key_grad_ref, value_grad_ref = rest[:5]
    dmix_ref, delta_ref, acc_ref, dkey_ref = rest[5:]
    step_id = pl.program_id(1)
    piece_id = step_id + first_piece
    nseq, _, strip, _ = lat_ref.shape
    rows = query_ref.shape[0]
    strips = KEY_BLOCK // strip
    per_piece = nseq // strips
    tall = PER_GROUP * rows

    @pl.when(step_id == 0)
    def _():
        if carried:
            dkey_ref[...] = carry_ref[...]
        else:
            dkey_ref[...] = jnp.zeros(dkey_ref.shape, F32)
        key_grad_ref[...] = jnp.zeros(key_grad_ref.shape, F32)
        value_grad_ref[...] = jnp.zeros(value_grad_ref.shape, F32)

    grads = grad_ref[...]
    for head, part in enumerate(expand_heads(grads, value_up_ref[...])):
        dmix_ref[head] = part.astype(BF16)
    value_grad_ref[...] += outer_heads([mixed_ref[0, 0, h] for h in range(PER_GROUP)], grads)
    dmix_all = dmix_ref[...].reshape(tall, LATENT).astype(F32)
    mixed_all = mixed_ref[0, 0].reshape(tall, LATENT).astype(F32)
    delta_ref[...] = jnp.sum(dmix_all * mixed_all, axis=1, keepdims=True)
    acc_ref[...] = jnp.zeros(acc_ref.shape, F32)
    starts = jnp.broadcast_to(start_ref[0][:, 0:1], (rows, KEY_BLOCK))

    def step(block, carry):
        keys, key_piece, first = load_keys(lat_ref, slot_ref, block, strips, per_piece)
        seen = visible(block, base_ref[piece_id], starts, rows)
        absorbed = abs_ref[0, 0].reshape(tall, LATENT)
        dmix = dmix_ref[...].reshape(tall, LATENT)
        probs = jnp.exp(masked(mm_nt(absorbed, keys) - lse_ref[0, 0][:, 0:1], seen, rows))
        d_scores = (probs * (mm_nt(dmix, keys) - delta_ref[...])).astype(BF16)
        acc_ref[...] += mm(d_scores, keys)
        d_keys = mm_tn(d_scores, absorbed) + mm_tn(probs.astype(BF16), dmix)
        for i in range(strips):
            dkey_ref[slot_ref[first + i], key_piece] += d_keys[i * strip : (i + 1) * strip]
        return carry

    lax.fori_loop(lo_ref[piece_id], hi_ref[piece_id], step, 0)
    d_abs = (acc_ref[...] * SCALE).astype(BF16).reshape(PER_GROUP, rows, LATENT)
    parts = [d_abs[h] for h in range(PER_GROUP)]
    dquery_ref[...] = shrink_heads(parts, key_up_ref[...]).astype(BF16)
    key_grad_ref[...] += outer_heads(parts, query_ref[...])

    @pl.when(step_id == pl.num_programs(1) - 1)
    def _():
        if carried:
            dlat_ref[...] = dkey_ref[...].astype(BF16)
        else:
            dlat_ref[...] = dkey_ref[:, first_piece:].astype(BF16)
            carry_ref[...] = dkey_ref[:, :first_piece]


def attention_specs(nseq, strip, first_piece):
    tall = PER_GROUP * strip

    def lat(pieces):
        return pl.BlockSpec((nseq, pieces, strip, LATENT), lambda g, p, *_: (0, 0, 0, g))

    table = pl.BlockSpec((1, strip, 128), lambda g, p, *_: (p + first_piece, 0, 0))
    rows = pl.BlockSpec((strip, GROUP_COLS), lambda g, p, *_: (p + first_piece, g))
    mine = pl.BlockSpec((strip, GROUP_COLS), lambda g, p, *_: (p, g))
    proj = pl.BlockSpec((LATENT, GROUP_COLS), lambda g, p, *_: (0, g))
    heads = pl.BlockSpec((1, 1, PER_GROUP, strip, LATENT), lambda g, p, *_: (g, p, 0, 0, 0))
    lse = pl.BlockSpec((1, 1, tall, 128), lambda g, p, *_: (g, p, 0, 0))
    return table, lat, rows, mine, proj, heads, lse


def kernel_params():
    return pltpu.CompilerParams(dimension_semantics=("arbitrary", "arbitrary"), vmem_limit_bytes=56 << 20)


def attention_cost(nseq, pieces, strip, matmuls):
    pairs = HEADS * pieces * strip * nseq * strip * 2
    return pl.CostEstimate(
        flops=2 * matmuls * pairs * LATENT, transcendentals=pairs, bytes_accessed=32 << 20
    )


def attention_forward(first_piece, pieces, tables, table, latents, queries, key_up, value_up):
    nseq, all_pieces, strip, _ = latents.shape
    tall = PER_GROUP * strip
    t_spec, lat_spec, row_spec, mine_spec, proj_spec, head_spec, lse_spec = attention_specs(nseq, strip, first_piece)
    head_shape = jax.ShapeDtypeStruct((GROUPS, pieces, PER_GROUP, strip, LATENT), BF16)
    return pl.pallas_call(
        functools.partial(forward_body, first_piece),
        name="attention_forward",
        grid_spec=pltpu.PrefetchScalarGridSpec(
            num_scalar_prefetch=len(tables),
            grid=(GROUPS, pieces),
            in_specs=[t_spec, lat_spec(all_pieces), row_spec, proj_spec, proj_spec],
            out_specs=[head_spec, head_spec, lse_spec, mine_spec],
            scratch_shapes=[
                pltpu.VMEM((tall, 1), F32),
                pltpu.VMEM((tall, 1), F32),
                pltpu.VMEM((tall, LATENT), F32),
            ],
        ),
        out_shape=[
            head_shape,
            head_shape,
            jax.ShapeDtypeStruct((GROUPS, pieces, tall, 128), F32),
            jax.ShapeDtypeStruct((pieces * strip, queries.shape[1]), BF16),
        ],
        compiler_params=kernel_params(),
        cost_estimate=attention_cost(nseq, pieces, strip, 2),
    )(*tables, table, latents, queries, key_up, value_up)


def attention_backward(
    first_piece, pieces, tables, table, latents, queries, key_up, value_up, absorbed, mixed, lse, grads, carry
):
    nseq, all_pieces, strip, lat_width = latents.shape
    tall = PER_GROUP * strip
    carried = carry is not None
    t_spec, lat_spec, row_spec, mine_spec, proj_spec, head_spec, lse_spec = attention_specs(nseq, strip, first_piece)
    seen_pieces = pieces if carried else all_pieces
    in_specs = [
        t_spec, lat_spec(all_pieces), row_spec, proj_spec, proj_spec, head_spec, head_spec, lse_spec, mine_spec,
    ]
    operands = [table, latents, queries, key_up, value_up, absorbed, mixed, lse, grads]
    out_specs = [mine_spec, lat_spec(pieces)]
    out_shape = [
        jax.ShapeDtypeStruct((pieces * strip, queries.shape[1]), BF16),
        jax.ShapeDtypeStruct((nseq, pieces, strip, lat_width), BF16),
    ]
    if carried:
        in_specs.append(lat_spec(pieces))
        operands.append(carry)
    else:
        out_specs.append(lat_spec(first_piece))
        out_shape.append(jax.ShapeDtypeStruct((nseq, first_piece, strip, lat_width), F32))
    proj_shape = jax.ShapeDtypeStruct(key_up.shape, F32)
    return pl.pallas_call(
        functools.partial(backward_body, first_piece, carried),
        name="attention_backward",
        grid_spec=pltpu.PrefetchScalarGridSpec(
            num_scalar_prefetch=len(tables),
            grid=(GROUPS, pieces),
            in_specs=in_specs,
            out_specs=[*out_specs, proj_spec, proj_spec],
            scratch_shapes=[
                pltpu.VMEM((PER_GROUP, strip, LATENT), BF16),
                pltpu.VMEM((tall, 1), F32),
                pltpu.VMEM((tall, LATENT), F32),
                pltpu.VMEM((nseq, seen_pieces, strip, LATENT), F32),
            ],
        ),
        out_shape=[*out_shape, proj_shape, proj_shape],
        compiler_params=kernel_params(),
        cost_estimate=attention_cost(nseq, pieces, strip, 5),
    )(*tables, *operands)


def row_starts(stretches, positions):
    entry = jnp.arange(stretches.shape[0], dtype=jnp.int32)
    ends = jnp.sum(jnp.where(entry[None, :] <= entry[:, None], stretches[None, :], 0), axis=1)
    firsts = (ends - stretches)[0::2]
    ends = ends[0::2]
    inside = (positions[:, None] >= firsts[None, :]) & (positions[:, None] < ends[None, :])
    first = jnp.sum(jnp.where(inside, firsts[None, :], 0), axis=1)
    return jnp.where(jnp.any(inside, axis=1), first, positions)


def inverse_rms(values):
    return lax.rsqrt(jnp.mean(values * values, axis=-1, keepdims=True) + NORM_EPS)


def norm_pull(values, inverse, gain, grads):
    scaled = gain * grads
    return inverse * scaled - values * (inverse**3) * jnp.mean(scaled * values, axis=-1, keepdims=True)


def my_half(shard):
    half = shard.shape[0] // 2
    return lax.dynamic_slice_in_dim(shard, lax.axis_index("core") * half, half, 0)


def swap_core(x):
    return lax.ppermute(x, "core", [(0, 1), (1, 0)])


def partner(x, step):
    return lax.ppermute(x, DP, [(i, i ^ step) for i in range(lax.axis_size(DP))])


def from_behind(x, step):
    nz = lax.axis_size("z")
    return lax.ppermute(x, "z", [(i, (i + step) % nz) for i in range(nz)])


def from_ahead(x, step):
    nz = lax.axis_size("z")
    return lax.ppermute(x, "z", [((i + step) % nz, i) for i in range(nz)])


def gather_dp(x):
    return [x] + [partner(x, step) for step in range(1, lax.axis_size(DP))]


def scatter_dp(parts):
    total = parts[0].astype(F32)
    for step in range(1, len(parts)):
        total = total + partner(parts[step].astype(BF16), step).astype(F32)
    return total


def after(x, *others):
    return lax.optimization_barrier((x, *others))[0]


def per_device(
    tokens, norm1_gain, w_query, w_latent, w_key_up, w_value_up, w_out, norm2_gain,
    w_gate, w_up, w_down, out_grad, seq_lengths,
):
    ndp = lax.axis_size(DP)
    nz = lax.axis_size("z")
    nseq = 2 * nz
    pieces, strip, width = tokens.shape[1:]
    span = strip * nseq
    rows = pieces * strip
    lat_width = GROUPS * LATENT
    my_z, my_core, my_dp = lax.axis_index("z"), lax.axis_index("core"), lax.axis_index(DP)
    my_seq = my_z * 2 + my_core
    shard = norm1_gain.shape[0]
    slice_ff = w_down.shape[0]
    wide_ff = -(-slice_ff // 128) * 128
    half = shard // 2

    gains = jnp.pad(jnp.concatenate([norm1_gain, norm2_gain])[None, :], ((0, 15), (0, lat_width - 2 * shard)))
    own_head = jnp.concatenate([my_half(w_latent), gains], axis=0)
    by_step = jnp.stack(gather_dp(own_head))
    other = swap_core(by_step)
    core_pair = jnp.where(my_core == 0, jnp.stack([by_step, other]), jnp.stack([other, by_step]))
    order = jnp.arange(ndp, dtype=jnp.int32) ^ my_dp
    head_pack = jnp.stack([lax.dynamic_index_in_dim(core_pair, order[i], 1, False) for i in range(ndp)])
    latent_w = head_pack[:, :, :half].reshape(width, lat_width)
    gains = head_pack[:, 0, half].astype(F32)
    gain_one = gains[:, :shard].reshape(1, width)
    gain_two = gains[:, shard : 2 * shard].reshape(1, width)
    pack = lax.all_gather(
        jnp.concatenate([my_half(w_query), my_half(w_key_up), my_half(w_value_up), my_half(w_out)], axis=0),
        CHIP,
        axis=0,
    )
    up_half = w_key_up.shape[0] // 2
    cuts = [0, half, half + up_half, half + 2 * up_half, 2 * half + 2 * up_half]
    query_w, key_w, value_w, out_w = (
        pack[:, a:b].reshape(-1, width) for a, b in zip(cuts[:-1], cuts[1:])
    )

    piece_base = jnp.arange(pieces, dtype=jnp.int32) * span + my_seq * strip
    row_pos = piece_base[:, None] + jnp.arange(strip, dtype=jnp.int32)[None, :]
    starts = row_starts(seq_lengths[0], row_pos.reshape(-1)).reshape(pieces, strip)
    seq_ids = jnp.arange(nseq, dtype=jnp.int32)
    slots = (seq_ids % 2 ^ my_core) * nz + (my_z - seq_ids // 2) % nz
    tables = (
        starts[:, 0] // KEY_BLOCK, (piece_base + strip + KEY_BLOCK - 1) // KEY_BLOCK, piece_base, slots,
    )
    table = jnp.broadcast_to(starts[:, :, None], (pieces, strip, 128))

    tok = tokens[0].reshape(rows, width).astype(F32)
    inv_one = inverse_rms(tok)
    normed = (tok * inv_one * gain_one).astype(BF16)
    latent = mm(normed, latent_w).astype(BF16).reshape(pieces, strip, lat_width)
    core_lat = jnp.stack([latent] + [from_behind(latent, step) for step in range(1, nz)])
    latents = jnp.concatenate([core_lat, swap_core(core_lat)], axis=0)
    queries = mm(normed, query_w).astype(BF16)

    def column_slices(w):
        parts = w.reshape(shard, ndp, slice_ff).transpose(1, 0, 2)
        return jnp.pad(parts, ((0, 0), (0, 0), (0, wide_ff - slice_ff)))

    sliced = jnp.stack([column_slices(w_gate), column_slices(w_up)], axis=1)
    sliced = lax.all_to_all(after(sliced, queries), DP, 0, 0, tiled=True)
    gate_w = sliced[:, 0].reshape(width, wide_ff)
    up_w = sliced[:, 1].reshape(width, wide_ff)
    down_w = jnp.pad(w_down, ((0, wide_ff - slice_ff), (0, 0)))

    grad_rows = out_grad[0].reshape(rows, width)
    grad_blocks = lax.all_gather(after(grad_rows, pack), DP, axis=0)
    grad_blocks = [lax.dynamic_index_in_dim(grad_blocks, order[i], 0, False) for i in range(ndp)]
    cut = pieces // 2
    chunks = [(cut, pieces - cut), (0, cut)]

    def rows_of(x, chunk):
        return x[chunk[0] * strip : (chunk[0] + chunk[1]) * strip]

    kept = []
    turn = queries
    for chunk in chunks:
        absorbed, mixed, lse, heads_out = attention_forward(
            *chunk, tables, table, latents, after(queries, turn), key_w, value_w
        )
        resid = rows_of(tok, chunk) + mm(heads_out, out_w)
        inv_two = inverse_rms(resid)
        normed_two = (resid * inv_two * gain_two).astype(BF16)
        kept.append((absorbed, mixed, lse, heads_out, resid, inv_two, gather_dp(normed_two)))
        turn = normed_two

    ff_state = []
    d_resids = []
    for chunk, state in zip(chunks, kept):
        size = chunk[1] * strip
        resid, inv_two, blocks = state[4:]
        normed_all = after(jnp.concatenate(blocks), turn)
        grad_all = jnp.concatenate([rows_of(x, chunk) for x in grad_blocks])
        gate = mm(normed_all, gate_w)
        up = mm(normed_all, up_w)
        sig = 1.0 / (1.0 + jnp.exp(-gate))
        silu = gate * sig
        hidden = (silu * up).astype(BF16)
        d_hidden = mm_nt(grad_all, down_w)
        d_gate = (d_hidden * up * (sig * (1.0 + gate * (1.0 - sig)))).astype(BF16)
        d_up = (d_hidden * silu).astype(BF16)
        d_part = (mm_nt(d_gate, gate_w) + mm_nt(d_up, up_w)).astype(BF16)
        turn = d_part
        d_normed_two = scatter_dp([d_part[i * size : (i + 1) * size] for i in range(ndp)])
        d_resids.append(
            rows_of(grad_rows, chunk).astype(F32) + norm_pull(resid, inv_two, gain_two, d_normed_two)
        )
        ff_state.append((normed_all, grad_all, hidden, d_gate, d_up))

    normed_all, grad_all, hidden, d_gate, d_up = (jnp.concatenate(parts) for parts in zip(*ff_state))
    down_grad = mm_tn(hidden, grad_all)[:slice_ff].astype(BF16)
    out_part = mm(hidden, down_w).astype(BF16)

    def tiles(x):
        *lead, a, b = x.shape
        x = x.reshape(*lead, a // 8, 8, b // 128, 128)
        return jnp.swapaxes(x, -2, -3).reshape(*lead, a * b // 1024, 8, 128)

    def untiled(x, a, b):
        lead = x.shape[:-3]
        x = x.reshape(*lead, a // 8, b // 128, 8, 128)
        return jnp.swapaxes(x, -2, -3).reshape(*lead, a, b)

    down_rows = -(-slice_ff // (8 * nseq)) * 8
    own_rows = -(-shard // (8 * nseq)) * 8

    def by_owner(grad):
        parts = grad.astype(BF16).reshape(ndp, shard, wide_ff)
        parts = jnp.pad(parts, ((0, 0), (0, own_rows * nseq - shard), (0, 0)))
        parts = parts.reshape(ndp, nseq, own_rows, wide_ff).transpose(1, 0, 2, 3)
        return tiles(parts.reshape(nseq, ndp * own_rows, wide_ff))

    ff_pack = jnp.concatenate(
        [
            tiles(jnp.pad(down_grad, ((0, down_rows * nseq - slice_ff), (0, 0))).reshape(nseq, down_rows, width)),
            by_owner(mm_tn(normed_all, d_gate)),
            by_owner(mm_tn(normed_all, d_up)),
        ],
        axis=1,
    )
    turn = ff_pack
    ff_pack = lax.psum_scatter(ff_pack, SEQ, scatter_dimension=0, tiled=True)[0]
    ff_reduced = ff_pack
    down_tiles = down_rows * width // 1024
    each = own_rows * wide_ff // 1024
    swap = ff_pack[down_tiles:].reshape(2, ndp, each, 8, 128)
    swap = lax.all_to_all(swap, DP, 1, 1, tiled=True)
    ff_pack = jnp.concatenate([ff_pack[:down_tiles], swap.reshape(2 * ndp * each, 8, 128)], axis=0)
    ff_pack = lax.all_gather(ff_pack, SEQ, axis=0)
    down_out = untiled(ff_pack[:, :down_tiles], down_rows, width).reshape(-1, width)[:slice_ff].astype(F32)
    halves = ff_pack[:, down_tiles:].reshape(nseq, 2, ndp, each, 8, 128)

    def joined(which):
        x = untiled(halves[:, which], own_rows, wide_ff)[..., :slice_ff]
        return x.transpose(0, 2, 1, 3).reshape(-1, ndp * slice_ff)[:shard].astype(F32)

    gate_out, up_out = joined(0), joined(1)

    def shares(grad):
        return grad.astype(BF16).reshape(ndp, 2, -1, grad.shape[1])

    def reduce_chip(grad):
        mine = lax.dynamic_index_in_dim(grad, my_core, 1, False)
        theirs = lax.dynamic_index_in_dim(grad, 1 - my_core, 1, False)
        chip = (mine.astype(F32) + swap_core(theirs).astype(F32)).astype(BF16)
        return scatter_dp([lax.dynamic_index_in_dim(chip, my_dp ^ step, 0, False) for step in range(ndp)])

    carry = None
    back = []
    for chunk, state, d_resid in zip(chunks, kept, d_resids):
        absorbed, mixed, lse, heads_out, resid = state[:5]
        d_heads = after(mm_nt(d_resid.astype(BF16), out_w).astype(BF16), turn)
        out = attention_backward(
            *chunk, tables, table, latents, queries, key_w, value_w, absorbed, mixed, lse, d_heads, carry
        )
        if carry is None:
            d_queries, d_lat, carry, key_grad, value_grad = out
        else:
            d_queries, d_lat, key_grad, value_grad = out
        core_sum = d_lat[:nz].astype(F32) + swap_core(d_lat[nz:]).astype(F32)
        send = core_sum.astype(BF16)
        d_latent = core_sum[0]
        for step in range(1, nz):
            d_latent = d_latent + from_ahead(send[step], step).astype(F32)
        d_latent = d_latent.astype(BF16).reshape(-1, lat_width)
        back.append((d_queries, d_latent, heads_out, d_resid, resid, key_grad, value_grad))
        turn = send

    back = back[::-1]
    d_queries, d_latent, heads_out, d_resid, resid = (jnp.concatenate(parts) for parts in list(zip(*back))[:5])
    size = rows // 2
    d_queries = after(d_queries, ff_reduced)
    key_grad = back[0][5] + back[1][5]
    value_grad = back[0][6] + back[1][6]
    out_grad_w = reduce_chip(shares(mm_tn(heads_out, d_resid.astype(BF16))))
    d_normed = mm_nt(d_queries, query_w) + mm_nt(d_latent, latent_w)
    tokens_grad = (d_resid + norm_pull(tok, inv_one, gain_one, d_normed)).astype(BF16)
    size = chunks[0][1] * strip
    block = [
        jnp.concatenate(
            [
                out_part[ndp * size + i * (rows - size) : ndp * size + (i + 1) * (rows - size)],
                out_part[i * size : (i + 1) * size],
            ]
        )
        for i in range(ndp)
    ]
    layer_out = (resid + scatter_dp(block)).astype(BF16)

    grad_pack = jnp.concatenate(
        [
            shares(mm_tn(normed, d_queries)),
            shares(key_grad),
            shares(value_grad),
            shares(mm_tn(normed, d_latent)).reshape(ndp, 2, -1, width),
        ],
        axis=2,
    )
    grad_pack = jnp.concatenate([reduce_chip(grad_pack), out_grad_w]).astype(BF16)
    own = after(tiles(grad_pack), ff_pack)
    own = own.reshape(nz, -1, 8, 128)
    own = lax.psum_scatter(own, "z", scatter_dimension=0, tiled=True)
    own = lax.all_gather(own[0], SEQ, axis=0)
    own = own.reshape(nz, 2, -1, 8, 128).transpose(1, 0, 2, 3, 4).reshape(2, -1, 8, 128)
    grad_pack = untiled(own, *grad_pack.shape).astype(F32)
    lat_rows = half * lat_width // width
    cuts = [half, half + up_half, half + 2 * up_half, half + 2 * up_half + lat_rows]
    query_out, key_out, value_out, latent_out, out_out = (
        grad_pack[:, a:b].reshape(-1, width) for a, b in zip([0, *cuts], [*cuts, grad_pack.shape[1]])
    )
    latent_out = latent_out.reshape(shard, lat_width)

    def weighed(weight, grad):
        return jnp.sum(weight.astype(F32) * grad, axis=1)

    gain_one_out = (weighed(w_query, query_out) + weighed(w_latent, latent_out)) / norm1_gain.astype(F32)
    gain_two_out = (weighed(w_gate, gate_out) + weighed(w_up, up_out)) / norm2_gain.astype(F32)

    shape = (1, pieces, strip, width)
    return (
        layer_out.reshape(shape), tokens_grad.reshape(shape), gain_one_out, query_out, latent_out, key_out,
        value_out, out_out, gain_two_out, gate_out, up_out, down_out,
    )


def solution(mesh):
    sizes = mesh.shape
    grid = Mesh(mesh.devices.reshape(sizes["dp"], sizes["seq"] // 2, 2), ("dp", "z", "core"))
    stream = P("dp", None, SEQ, None)
    vector, matrix = P("dp"), P("dp", None)
    in_specs = (
        stream, vector, matrix, matrix, matrix, matrix, matrix, vector, matrix, matrix, matrix, stream, matrix,
    )
    out_specs = (
        stream, stream, vector, matrix, matrix, matrix, matrix, matrix, vector, matrix, matrix, matrix,
    )
    return jax.shard_map(per_device, mesh=grid, in_specs=in_specs, out_specs=out_specs, check_vma=False)
```

time: 1130 us -> 486 us (0.43)
  waiting for transfers between devices: 584 us -> 151 us
  blocking collectives: 289 us -> 0 us
  matrix products: 145 us -> 40 us
  starting transfers between devices: 0.89 us -> 67.8 us
  Pallas kernels: 0 us -> 64.2 us
  local copies, waits for them, and re-layouts: 51.7 us -> 85.7 us
  other arithmetic: 26.2 us -> 45 us
    reduce_scatter x9 -> x2, waiting for transfers between devices: 348 us -> 20.6 us  [the longest x1 20.6 us: per_device(): own = lax.psum_scatter(own, 'z', scatter_dimension=0, tiled=True)]
    psum x1 -> x0, blocking collectives: 236 us -> none  [per_device(): lax.psum((shares[0], shares[1], shares[2], shares[3], shares[4], shares[5...]
    all_gather x7 -> x4, waiting for transfers between devices: 232 us -> 0.01 us  [the longest x1 0.01 us: per_device(): grad_blocks = lax.all_gather(after(grad_rows, pack), DP, axis=0)]
    ppermute x0 -> x39, waiting for transfers between devices: none -> 126 us  [the longest x24 78.9 us: partner(): lax.ppermute(x, DP, [(i, i ^ step) for i in range(lax.axis_size(DP))])]
    dot_general x36 -> x25, matrix products: 145 us -> 40 us  [the longest x9 16.4 us: mm(): return jnp.dot(a, b, preferred_element_type=F32)]
    pallas_call x0 -> x4, Pallas kernels: none -> 64.2 us  [the longest x2 34.1 us: attention_forward(): pl.pallas_call(functools.partial(forward_body, first_piece), name='attent...]
    ppermute x0 -> x39, starting transfers between devices: none -> 58.4 us  [the longest x24 35.7 us: partner(): lax.ppermute(x, DP, [(i, i ^ step) for i in range(lax.axis_size(DP))])]
    all_gather x4 -> x0, blocking collectives: 44.2 us -> none  [the longest x1 14 us: per_device(): lax.all_gather(w_key_up, 'dp', axis=0, tiled=True)]
  transfers between devices with their start and end apart: 16 -> 47, of which waited for: 14 -> 22; matrix products, arithmetic and copies ran while one was open for 10% -> 26% of each run, Pallas kernels for 0% -> 13%
where the time goes in v1:
time: 486 us; the launch traced here: 477 us
  waiting for transfers between devices  151 us (31%)
  local copies, waits for them, and re-layouts  85.7 us (18%)
  starting transfers between devices  67.8 us (14%)
  Pallas kernels  64.2 us (13%)
  other arithmetic  45 us (9%)
  matrix products  40 us (8%)
  between operations  23.4 us (5%)
    ppermute x24, waiting for transfers between devices, partner(): lax.ppermute(x, DP, [(i, i ^ step) for i in range(lax.axis_size(DP))])  78.9 us
    ppermute x24, starting transfers between devices, partner(): lax.ppermute(x, DP, [(i, i ^ step) for i in range(lax.axis_size(DP))])  35.7 us
    pallas_call x2, Pallas kernels, attention_forward(): pl.pallas_call(functools.partial(forward_body, first_piece), name='attent...  34.1 us
    pallas_call x2, Pallas kernels, attention_backward(): pl.pallas_call(functools.partial(backward_body, first_piece, carried), na...  30.1 us
    ppermute x6, waiting for transfers between devices, from_ahead(): return lax.ppermute(x, 'z', [((i + step) % nz, i) for i in range(nz)])  30 us
    unnamed x160, local copies, waits for them, and re-layouts  28.5 us
    reduce_scatter x1, waiting for transfers between devices, per_device(): own = lax.psum_scatter(own, 'z', scatter_dimension=0, tiled=True)  20.6 us
    convert_element_type x4, local copies, waits for them, and re-layouts, joined(): x.transpose(0, 2, 1, 3).reshape(-1, ndp * slice_ff)[:shard].astype(F32)  17.5 us
  transfers between devices with their start and end apart: 47, of which 22 were waited for; matrix products, arithmetic and copies ran while one was open for 26% of the time, Pallas kernels for 13%

profile of v1, /device:TPU:0, one launch (start us, length us, event | category | flops | bytes accessed | tf_op | source)
XLA Modules:
  0.0 477.2 jit_solution(5269928590450821129)
XLA Ops:
  46.0 10.1 %collective-permute-done.5 = bf16[4,64,512]{2,1,0:T(8,128)(2,1)S(1)} collective-permute-done((bf16[4,64,512]{2,1,0:T(8,128)(2,1)S(1)}, bf16[4,64,512]{2,1,0:T(8,128)(2,1)S(1)}, u32[]{:S(2)}, u32[]{:S(2)}) %collective-permute-start.5) | collective-permute-done | bytes 262176 | tf_op jit(solution)/shard_map/ppermute | solution.py:338
  72.4 4.7 all-to-all-start
  77.9 20.9 %attention_forward.2 = (bf16[2,2,8,64,256]{4,3,2,1,0:T(8,128)(2,1)}, bf16[2,2,8,64,256]{4,3,2,1,0:T(8,128)(2,1)}, f32[2,2,512,128]{3,2,1,0:T(8,128)}, bf16[128,1024]{1,0:T(8,128)(2,1)}) custom-call(s32[4]{0:T(128)} %get-tuple-element.163.lo_ref.refs_0_, s32[4]{0:T(128)} %get-tuple-element.162.hi_ref.refs_1_, s32[4]{0:T(128)} %copy-done.59, ...), custom_call_target="tpu_custom_call" | custom-call | flops 2147483648 | bytes 33554432 | tf_op jit(solution)/shard_map/attention_forward/pallas_call | solution.py:234
  100.5 5.4 %collective-permute-start.10 = (bf16[128,1024]{1,0:T(8,128)(2,1)S(1)}, bf16[128,1024]{1,0:T(8,128)(2,1)S(1)}, u32[]{:S(2)}, u32[]{:S(2)}) collective-permute-start(bf16[128,1024]{1,0:T(8,128)(2,1)S(1)} %multiply_convert_fusion.7), channel_id=1, source_target_pairs={{0,24},{8,16},{16,8},{24,0},{1,25},{9,17},{17,9},{25,1},{2,26},{10... | collective-permute-start | bytes 786440 | tf_op jit(solution)/shard_map/ppermute | solution.py:333
  106.6 13.2 %attention_forward.3 = (bf16[2,2,8,64,256]{4,3,2,1,0:T(8,128)(2,1)}, bf16[2,2,8,64,256]{4,3,2,1,0:T(8,128)(2,1)}, f32[2,2,512,128]{3,2,1,0:T(8,128)}, bf16[128,1024]{1,0:T(8,128)(2,1)}) custom-call(s32[4]{0:T(128)} %get-tuple-element.163.lo_ref.refs_0_, s32[4]{0:T(128)} %get-tuple-element.162.hi_ref.refs_1_, s32[4]{0:T(128)} %copy-done.59, ...), custom_call_target="tpu_custom_call" | custom-call | flops 2147483648 | bytes 33554432 | tf_op jit(solution)/shard_map/attention_forward/pallas_call | solution.py:234
  122.2 5.4 %collective-permute-start.13 = (bf16[128,1024]{1,0:T(8,128)(2,1)S(1)}, bf16[128,1024]{1,0:T(8,128)(2,1)S(1)}, u32[]{:S(2)}, u32[]{:S(2)}) collective-permute-start(bf16[128,1024]{1,0:T(8,128)(2,1)S(1)} %multiply_convert_fusion.6), channel_id=1, source_target_pairs={{0,24},{8,16},{16,8},{24,0},{1,25},{9,17},{17,9},{25,1},{2,26},{10... | collective-permute-start | bytes 786440 | tf_op jit(solution)/shard_map/ppermute | solution.py:333
  127.6 9.1 %collective-permute-done.10 = bf16[128,1024]{1,0:T(8,128)(2,1)S(1)} collective-permute-done((bf16[128,1024]{1,0:T(8,128)(2,1)S(1)}, bf16[128,1024]{1,0:T(8,128)(2,1)S(1)}, u32[]{:S(2)}, u32[]{:S(2)}) %collective-permute-start.10) | collective-permute-done | bytes 262176 | tf_op jit(solution)/shard_map/ppermute | solution.py:333
  144.7 4.5 collective-permute-done.13
  149.2 4.2 collective-permute-done.12
  207.6 4.4 collective-permute-done.18
  212.0 5.6 %collective-permute-done.22 = bf16[128,1024]{1,0:T(8,128)(2,1)S(1)} collective-permute-done((bf16[128,1024]{1,0:T(8,128)(2,1)S(1)}, bf16[128,1024]{1,0:T(8,128)(2,1)S(1)}, u32[]{:S(2)}, u32[]{:S(2)}) %collective-permute-start.22) | collective-permute-done | bytes 262176 | tf_op jit(solution)/shard_map/ppermute | solution.py:333
  217.6 4.2 collective-permute-done.21
  226.0 17.4 %attention_backward.2 = (bf16[128,1024]{1,0:T(8,128)(2,1)}, bf16[8,2,64,512]{3,2,1,0:T(8,128)(2,1)}, f32[8,2,64,512]{3,2,1,0:T(8,128)}, f32[256,1024]{1,0:T(8,128)}, f32[256,1024]{1,0:T(8,128)}) custom-call(s32[4]{0:T(128)} %get-tuple-element.163.lo_ref.refs_0_, s32[4]{0:T(128)} %get-tuple-element.162.hi_ref.refs_1_, s32[4]{0:T(128)} %copy-done.59, ...), custom_call_target="tpu_custom_call" | custom-call | flops 5368709120 | bytes 33554432 | tf_op jit(solution)/shard_map/attention_backward/pallas_call | solution.py:283
  249.8 4.5 all-to-all-start.1
  262.5 12.7 %attention_backward.3 = (bf16[128,1024]{1,0:T(8,128)(2,1)}, bf16[8,2,64,512]{3,2,1,0:T(8,128)(2,1)}, f32[256,1024]{1,0:T(8,128)}, f32[256,1024]{1,0:T(8,128)}) custom-call(s32[4]{0:T(128)} %get-tuple-element.163.lo_ref.refs_0_, s32[4]{0:T(128)} %get-tuple-element.162.hi_ref.refs_1_, s32[4]{0:T(128)} %copy-done.59, s32[8]{0:T(128)} %fusion.66.slot_ref.refs_3_, ...), custom_call_target="tpu_custom_call" | custom-call | flops 5368709120 | bytes 33554432 | tf_op jit(solution)/shard_map/attention_backward/pallas_call | solution.py:283
  279.5 7.3 %collective-permute-start.29 = (bf16[2,64,512]{2,1,0:T(8,128)(2,1)S(1)}, bf16[2,64,512]{2,1,0:T(8,128)(2,1)S(1)}, u32[]{:S(2)}, u32[]{:S(2)}) collective-permute-start(bf16[2,64,512]{2,1,0:T(8,128)(2,1)S(1)} %get-tuple-element.137), channel_id=1, source_target_pairs={{4,0},{6,2},{0,4},{2,6},{5,1},{7,3},{1,5},{3,7},{12,8},{14,10},{8,... | collective-permute-start | bytes 393224 | tf_op jit(solution)/shard_map/ppermute | solution.py:343
  297.0 6.3 %collective-permute-done.29 = bf16[2,64,512]{2,1,0:T(8,128)(2,1)S(1)} collective-permute-done((bf16[2,64,512]{2,1,0:T(8,128)(2,1)S(1)}, bf16[2,64,512]{2,1,0:T(8,128)(2,1)S(1)}, u32[]{:S(2)}, u32[]{:S(2)}) %collective-permute-start.29) | collective-permute-done | bytes 131104 | tf_op jit(solution)/shard_map/ppermute | solution.py:343
  304.3 6.0 %collective-permute-done.27 = bf16[2,64,512]{2,1,0:T(8,128)(2,1)S(1)} collective-permute-done((bf16[2,64,512]{2,1,0:T(8,128)(2,1)S(1)}, bf16[2,64,512]{2,1,0:T(8,128)(2,1)S(1)}, u32[]{:S(2)}, u32[]{:S(2)}) %collective-permute-start.27) | collective-permute-done | bytes 131104 | tf_op jit(solution)/shard_map/ppermute | solution.py:343
  310.2 17.7 %collective-permute-done.26 = bf16[2,64,512]{2,1,0:T(8,128)(2,1)S(1)} collective-permute-done((bf16[2,64,512]{2,1,0:T(8,128)(2,1)S(1)}, bf16[2,64,512]{2,1,0:T(8,128)(2,1)S(1)}, u32[]{:S(2)}, u32[]{:S(2)}) %collective-permute-start.26) | collective-permute-done | bytes 131104 | tf_op jit(solution)/shard_map/ppermute | solution.py:343
  359.8 26.8 %collective-permute-done.37 = bf16[128,1024]{1,0:T(8,128)(2,1)} collective-permute-done((bf16[128,1024]{1,0:T(8,128)(2,1)}, bf16[128,1024]{1,0:T(8,128)(2,1)}, u32[]{:S(2)}, u32[]{:S(2)}) %collective-permute-start.37) | collective-permute-done | bytes 262176 | tf_op jit(solution)/shard_map/ppermute | solution.py:333
  399.7 20.6 %reduce-scatter.5.cloned.1.call-done = bf16[1,96,8,128]{3,2,1,0:T(8,128)(2,1)} async-done(((bf16[4,96,8,128]{3,2,1,0:T(8,128)(2,1)}), bf16[1,96,8,128]{3,2,1,0:T(8,128)(2,1)}) %reduce-scatter.5.cloned.1.call-update) | async-done | bytes 196624 | tf_op jit(solution)/shard_map/reduce_scatter | solution.py:585
  422.1 10.7 %collective-permute-done.14 = bf16[256,1024]{1,0:T(8,128)(2,1)S(1)} collective-permute-done((bf16[256,1024]{1,0:T(8,128)(2,1)S(1)}, bf16[256,1024]{1,0:T(8,128)(2,1)S(1)}, u32[]{:S(2)}, u32[]{:S(2)}) %collective-permute-start.14) | collective-permute-done | bytes 524320 | tf_op jit(solution)/shard_map/ppermute | solution.py:333
  441.0 5.1 %reshape.372 = f32[256,2816]{1,0:T(8,128)} reshape(f32[8,32,4,704]{3,2,1,0:T(4,128)} %copy.79) | data formatting | bytes 5767168 | tf_op jit(solution)/shard_map/convert_element_type | solution.py:518
  451.7 4.9 %reshape.373 = f32[256,2816]{1,0:T(8,128)} reshape(f32[8,32,4,704]{3,2,1,0:T(4,128)} %copy.80) | data formatting | bytes 5767168 | tf_op jit(solution)/shard_map/convert_element_type | solution.py:518
  (384 shorter events, 222.0 us)
Async XLA Ops:
  7.2 53.6 %all-gather.10.cloned.1.call-start = ((), (), s32[]{:S(2)}) async-start(), calls=%async_computation.7 | async-start | bytes 5898240 | tf_op jit(solution)/shard_map/all_gather | solution.py:390
  10.2 157.5 %all-gather.12.cloned.1.call-start = ((), (), s32[]{:S(2)}) async-start(), calls=%async_computation.8 | async-start | bytes 2621440 | tf_op jit(solution)/shard_map/all_gather | solution.py:430
  36.6 19.4 %collective-permute-start.5 = (bf16[4,64,512]{2,1,0:T(8,128)(2,1)S(1)}, bf16[4,64,512]{2,1,0:T(8,128)(2,1)S(1)}, u32[]{:S(2)}, u32[]{:S(2)}) collective-permute-start(bf16[4,64,512]{2,1,0:T(8,128)(2,1)S(1)} %bitcast.312), channel_id=1, source_target_pairs={{0,4},{2,6},{4,0},{6,2},{1,5},{3,7},{5,1},{7,3},{8,12},{10,14},{12... | collective-permute-start | bytes 786440 | tf_op jit(solution)/shard_map/ppermute | solution.py:338
  72.4 82.1 %all-to-all-start = ((bf16[4,2,256,768]{2,3,1,0:T(8,128)(2,1)}), bf16[4,2,256,768]{2,3,1,0:T(8,128)(2,1)}, u32[]{:S(2)}, u32[]{:S(2)}) async-start(bf16[4,2,256,768]{2,3,1,0:T(8,128)(2,1)} %copy.70), calls=%async_computation | async-start | bytes 6291456 | tf_op jit(solution)/shard_map/all_to_all | solution.py:424
  77.1 170.8 %reduce-scatter.3.cloned.1.call-start = ((), (), s32[]{:S(2)}) async-start(), calls=%async_computation.4 | async-start | bytes 5160960 | tf_op jit(solution)/shard_map/reduce_scatter | solution.py:505
  100.5 36.2 %collective-permute-start.10 = (bf16[128,1024]{1,0:T(8,128)(2,1)S(1)}, bf16[128,1024]{1,0:T(8,128)(2,1)S(1)}, u32[]{:S(2)}, u32[]{:S(2)}) collective-permute-start(bf16[128,1024]{1,0:T(8,128)(2,1)S(1)} %multiply_convert_fusion.7), channel_id=1, source_target_pairs={{0,24},{8,16},{16,8},{24,0},{1,25},{9,17},{17,9},{25,1},{2,26},{10... | collective-permute-start | bytes 786440 | tf_op jit(solution)/shard_map/ppermute | solution.py:333
  105.9 35.4 %collective-permute-start.9 = (bf16[128,1024]{1,0:T(8,128)(2,1)S(1)}, bf16[128,1024]{1,0:T(8,128)(2,1)S(1)}, u32[]{:S(2)}, u32[]{:S(2)}) collective-permute-start(bf16[128,1024]{1,0:T(8,128)(2,1)S(1)} %multiply_convert_fusion.7), channel_id=1, source_target_pairs={{0,16},{8,24},{16,0},{24,8},{1,17},{9,25},{17,1},{25,9},{2,18},{10... | collective-permute-start | bytes 786440 | tf_op jit(solution)/shard_map/ppermute | solution.py:333
  105.9 36.7 %collective-permute-start.8 = (bf16[128,1024]{1,0:T(8,128)(2,1)S(1)}, bf16[128,1024]{1,0:T(8,128)(2,1)S(1)}, u32[]{:S(2)}, u32[]{:S(2)}) collective-permute-start(bf16[128,1024]{1,0:T(8,128)(2,1)S(1)} %multiply_convert_fusion.7), channel_id=1, source_target_pairs={{0,8},{8,0},{16,24},{24,16},{1,9},{9,1},{17,25},{25,17},{2,10},{10... | collective-permute-start | bytes 786440 | tf_op jit(solution)/shard_map/ppermute | solution.py:333
  122.2 27.0 %collective-permute-start.13 = (bf16[128,1024]{1,0:T(8,128)(2,1)S(1)}, bf16[128,1024]{1,0:T(8,128)(2,1)S(1)}, u32[]{:S(2)}, u32[]{:S(2)}) collective-permute-start(bf16[128,1024]{1,0:T(8,128)(2,1)S(1)} %multiply_convert_fusion.6), channel_id=1, source_target_pairs={{0,24},{8,16},{16,8},{24,0},{1,25},{9,17},{17,9},{25,1},{2,26},{10... | collective-permute-start | bytes 786440 | tf_op jit(solution)/shard_map/ppermute | solution.py:333
  127.6 25.8 %collective-permute-start.12 = (bf16[128,1024]{1,0:T(8,128)(2,1)S(1)}, bf16[128,1024]{1,0:T(8,128)(2,1)S(1)}, u32[]{:S(2)}, u32[]{:S(2)}) collective-permute-start(bf16[128,1024]{1,0:T(8,128)(2,1)S(1)} %multiply_convert_fusion.6), channel_id=1, source_target_pairs={{0,16},{8,24},{16,0},{24,8},{1,17},{9,25},{17,1},{25,9},{2,18},{10... | collective-permute-start | bytes 786440 | tf_op jit(solution)/shard_map/ppermute | solution.py:333
  201.2 20.6 %collective-permute-start.21 = (bf16[128,1024]{1,0:T(8,128)(2,1)S(1)}, bf16[128,1024]{1,0:T(8,128)(2,1)S(1)}, u32[]{:S(2)}, u32[]{:S(2)}) collective-permute-start(bf16[128,1024]{1,0:T(8,128)(2,1)S(1)} %get-tuple-element.124), channel_id=1, source_target_pairs={{0,16},{8,24},{16,0},{24,8},{1,17},{9,25},{17,1},{25,9},{2,18},{10... | collective-permute-start | bytes 786440 | tf_op jit(solution)/shard_map/ppermute | solution.py:333
  254.3 136.2 %all-gather.14.cloned.1.call-start = ((), (), s32[]{:S(2)}) async-start(), calls=%async_computation.9 | async-start | bytes 5160960 | tf_op jit(solution)/shard_map/all_gather | solution.py:512
  262.5 157.9 %reduce-scatter.5.cloned.1.call-start = ((), (), s32[]{:S(2)}) async-start(), calls=%async_computation.5 | async-start | bytes 983040 | tf_op jit(solution)/shard_map/reduce_scatter | solution.py:585
  279.5 23.8 %collective-permute-start.29 = (bf16[2,64,512]{2,1,0:T(8,128)(2,1)S(1)}, bf16[2,64,512]{2,1,0:T(8,128)(2,1)S(1)}, u32[]{:S(2)}, u32[]{:S(2)}) collective-permute-start(bf16[2,64,512]{2,1,0:T(8,128)(2,1)S(1)} %get-tuple-element.137), channel_id=1, source_target_pairs={{4,0},{6,2},{0,4},{2,6},{5,1},{7,3},{1,5},{3,7},{12,8},{14,10},{8,... | collective-permute-start | bytes 393224 | tf_op jit(solution)/shard_map/ppermute | solution.py:343
  293.4 34.6 %collective-permute-start.26 = (bf16[2,64,512]{2,1,0:T(8,128)(2,1)S(1)}, bf16[2,64,512]{2,1,0:T(8,128)(2,1)S(1)}, u32[]{:S(2)}, u32[]{:S(2)}) collective-permute-start(bf16[2,64,512]{2,1,0:T(8,128)(2,1)S(1)} %get-tuple-element.134), channel_id=1, source_target_pairs={{4,0},{6,2},{0,4},{2,6},{5,1},{7,3},{1,5},{3,7},{12,8},{14,10},{8,... | collective-permute-start | bytes 393224 | tf_op jit(solution)/shard_map/ppermute | solution.py:343
  293.4 34.6 %collective-permute-start.25 = (bf16[2,64,512]{2,1,0:T(8,128)(2,1)S(1)}, bf16[2,64,512]{2,1,0:T(8,128)(2,1)S(1)}, u32[]{:S(2)}, u32[]{:S(2)}) collective-permute-start(bf16[2,64,512]{2,1,0:T(8,128)(2,1)S(1)} %get-tuple-element.132), channel_id=1, source_target_pairs={{2,0},{4,2},{6,4},{0,6},{3,1},{5,3},{7,5},{1,7},{10,8},{12,10},{14... | collective-permute-start | bytes 393224 | tf_op jit(solution)/shard_map/ppermute | solution.py:343
  355.0 32.8 %collective-permute-start.34 = (bf16[256,1024]{1,0:T(8,128)(2,1)}, bf16[256,1024]{1,0:T(8,128)(2,1)}, u32[]{:S(2)}, u32[]{:S(2)}) collective-permute-start(bf16[256,1024]{1,0:T(8,128)(2,1)} %get-tuple-element.101), channel_id=1, source_target_pairs={{0,24},{8,16},{16,8},{24,0},{1,25},{9,17},{17,9},{25,1},{2,26},{10... | collective-permute-start | bytes 1572872 | tf_op jit(solution)/shard_map/ppermute | solution.py:333
  355.7 32.1 %collective-permute-start.33 = (bf16[256,1024]{1,0:T(8,128)(2,1)}, bf16[256,1024]{1,0:T(8,128)(2,1)}, u32[]{:S(2)}, u32[]{:S(2)}) collective-permute-start(bf16[256,1024]{1,0:T(8,128)(2,1)} %get-tuple-element.102), channel_id=1, source_target_pairs={{0,16},{8,24},{16,0},{24,8},{1,17},{9,25},{17,1},{25,9},{2,18},{10... | collective-permute-start | bytes 1572872 | tf_op jit(solution)/shard_map/ppermute | solution.py:333
  355.7 32.1 %collective-permute-start.32 = (bf16[256,1024]{1,0:T(8,128)(2,1)S(1)}, bf16[256,1024]{1,0:T(8,128)(2,1)}, u32[]{:S(2)}, u32[]{:S(2)}) collective-permute-start(bf16[256,1024]{1,0:T(8,128)(2,1)S(1)} %get-tuple-element.100), channel_id=1, source_target_pairs={{0,8},{8,0},{16,24},{24,16},{1,9},{9,1},{17,25},{25,17},{2,10},{10... | collective-permute-start | bytes 1572872 | tf_op jit(solution)/shard_map/ppermute | solution.py:333
  358.5 28.0 %collective-permute-start.37 = (bf16[128,1024]{1,0:T(8,128)(2,1)}, bf16[128,1024]{1,0:T(8,128)(2,1)}, u32[]{:S(2)}, u32[]{:S(2)}) collective-permute-start(bf16[128,1024]{1,0:T(8,128)(2,1)} %get-tuple-element.121), channel_id=1, source_target_pairs={{0,16},{8,24},{16,0},{24,8},{1,17},{9,25},{17,1},{25,9},{2,18},{10... | collective-permute-start | bytes 786440 | tf_op jit(solution)/shard_map/ppermute | solution.py:333
  358.5 28.0 %collective-permute-start.36 = (bf16[128,1024]{1,0:T(8,128)(2,1)}, bf16[128,1024]{1,0:T(8,128)(2,1)}, u32[]{:S(2)}, u32[]{:S(2)}) collective-permute-start(bf16[128,1024]{1,0:T(8,128)(2,1)} %get-tuple-element.119), channel_id=1, source_target_pairs={{0,8},{8,0},{16,24},{24,16},{1,9},{9,1},{17,25},{25,17},{2,10},{10... | collective-permute-start | bytes 786440 | tf_op jit(solution)/shard_map/ppermute | solution.py:333
  390.6 72.7 %all-gather.8.cloned.1.call-start = ((), (), s32[]{:S(2)}) async-start(), calls=%async_computation.6 | async-start | bytes 1769472 | tf_op jit(solution)/shard_map/all_gather | solution.py:586
  396.1 25.9 %collective-permute-start.16 = (bf16[256,1024]{1,0:T(8,128)(2,1)}, bf16[256,1024]{1,0:T(8,128)(2,1)S(1)}, u32[]{:S(2)}, u32[]{:S(2)}) collective-permute-start(bf16[256,1024]{1,0:T(8,128)(2,1)} %pad_maximum_fusion.19), channel_id=1, source_target_pairs={{0,24},{8,16},{16,8},{24,0},{1,25},{9,17},{17,9},{25,1},{2,26},{10... | collective-permute-start | bytes 1572872 | tf_op jit(solution)/shard_map/ppermute | solution.py:333
  399.1 23.0 %collective-permute-start.15 = (bf16[256,1024]{1,0:T(8,128)(2,1)}, bf16[256,1024]{1,0:T(8,128)(2,1)S(1)}, u32[]{:S(2)}, u32[]{:S(2)}) collective-permute-start(bf16[256,1024]{1,0:T(8,128)(2,1)} %pad_maximum_fusion.18), channel_id=1, source_target_pairs={{0,16},{8,24},{16,0},{24,8},{1,17},{9,25},{17,1},{25,9},{2,18},{10... | collective-permute-start | bytes 1572872 | tf_op jit(solution)/shard_map/ppermute | solution.py:333
  (93 other events, 812.7 us)
Sparse Core Ops, SparseCore 0:
  10.5 43.8 all-gather.9
  66.5 83.0 all-gather.11
  192.2 55.2 reduce-scatter.2
  262.6 76.1 all-gather.13
  390.7 29.6 reduce-scatter.4
  421.9 24.3 all-gather.7
